TPU v7x, 512 devices: a whole 4x4x16 slice. The times are simulated.
512 devices in a mesh: sector: 16 (over y, x_lo, core), dom: 32 (over z, x_hi).
Axes of the slice: x: 4 (x_hi: 2, x_lo: 2; x = x_hi * 2 + x_lo), y: 4, z: 16, core: 2. Of those that a mesh axis runs over, the one named last changes fastest.
Arguments:
- amplitudes: float32 [64, 48], replicated, may hold values from -0.3 to 0.3
- mode_shapes: float32 [48, 3, 524288], P(None, None, ('sector', 'dom')), may hold values from -6 to 6
- shape_grads: float32 [8, 3, 524288], P(None, None, ('sector', 'dom')), may hold values from -2.4 to 2.4
- lame_params: float32 [2, 524288], P(None, ('sector', 'dom')), may hold values from 0.5 to 2
- connectivity: int32 [8, 524288], P(None, ('sector', 'dom')), may hold values from -1 to 1791, as said below
- dom_sends: int32 [2, 131072], P(None, ('sector', 'dom')), may hold values from -1 to 1023, as said below
- sector_sends: int32 [2, 65536], P(None, ('sector', 'dom')), may hold values from -1 to 1023, as said below
Outputs:
- nodal_force: float32 [64, 3, 524288], P(None, None, ('sector', 'dom'))
- modal_force: float32 [64, 48], replicated
Inputs may be any that keep to these rules, and one draw needn't show every extreme that they name: `connectivity`: in each device's block, the live elements come first and the padding element slots after them hold -1 in all 8 rows; a live slot names a slot of the device's extended table. Some device has all 1024 slots live. `dom_sends`: each device's row lists its own node numbers first, then -1; a row holds 128 to 256 live entries, and some row is full. `sector_sends`: each device's row lists its own node numbers first, then -1; a row holds 64 to 128 live entries, and some row is full.
All inputs are finite; a program needn't handle non-finite values.
Results may differ from a plain program's by a relative error of at most 0.0003.
Values sent between devices are 32-bit elements; how exact they have to be, the bound alone decides.
A program may use at most 64 MiB of HBM per device.

v0:
```python
import math
import jax
import jax.numpy as jnp
from jax import lax
from jax.sharding import PartitionSpec as P


def padded(cells, sides, width, closed):
    for axis, dim in sides:
        count = lax.axis_size(axis)
        ends = count if closed else count - 1
        head = lax.slice_in_dim(cells, 0, width, axis=dim)
        tail = lax.slice_in_dim(cells, cells.shape[dim] - width, cells.shape[dim], axis=dim)
        cells = jnp.concatenate(
            [
                lax.ppermute(tail, axis, [(i, (i + 1) % count) for i in range(ends)]),
                cells,
                lax.ppermute(head, axis, [((i + 1) % count, i) for i in range(ends)]),
            ],
            axis=dim,
        )
    return cells


def take_slots(node_table, send_lists):
    slot_width = node_table.shape[1]
    slot_index = jnp.where(send_lists < 0, slot_width, send_lists).reshape(-1)
    return jnp.take(node_table, slot_index, axis=1, mode="fill", fill_value=0.0)


def add_slots(node_table, send_lists, add_values):
    slot_width = node_table.shape[1]
    slot_index = jnp.where(send_lists < 0, slot_width, send_lists).reshape(-1)
    return node_table.at[:, slot_index].add(add_values, mode="drop")


def element_forces(accum, extended, connect, gradients, lame):
    ext_width = extended.shape[1]
    combo_total = extended.shape[0] // 3
    elem_total = connect.shape[1]
    slot_index = jnp.where(connect < 0, ext_width, connect).reshape(-1)
    corners = jnp.take(extended, slot_index, axis=1, mode="fill", fill_value=0.0).reshape(
        combo_total, 3, 8, elem_total
    )
    gradient = jnp.zeros((combo_total, 3, 3, elem_total), extended.dtype)
    for corner in range(8):
        gradient = gradient + corners[:, :, None, corner, :] * gradients[corner][None, None, :, :]
    quadratic = jnp.sum(gradient[:, :, :, None, :] * gradient[:, :, None, :, :], axis=1)
    green_strain = 0.5 * (gradient + jnp.swapaxes(gradient, 1, 2) + quadratic)
    strain_trace = green_strain[:, 0, 0] + green_strain[:, 1, 1] + green_strain[:, 2, 2]
    identity = jnp.eye(3, dtype=extended.dtype)[None, :, :, None]
    stress = lame[0] * strain_trace[:, None, None, :] * identity + 2.0 * lame[1] * green_strain
    piola = stress + jnp.sum(gradient[:, :, :, None, :] * stress[:, None, :, :, :], axis=2)
    corner_forces = jnp.stack(
        [jnp.sum(piola * gradients[corner][None, None, :, :], axis=2) for corner in range(8)],
        axis=2,
    )
    return accum.at[:, slot_index].add(
        corner_forces.reshape(3 * combo_total, 8 * elem_total), mode="drop"
    )


def outer_ends(ext_rows, slot_width):
    return jnp.concatenate([ext_rows[:, :slot_width], ext_rows[:, 3 * slot_width :]], axis=1)


def local(amplitudes, mode_shapes, shape_grads, lame_params, connectivity, dom_sends, sector_sends):
    modes_total, _, node_total = mode_shapes.shape
    combo_total = amplitudes.shape[0]
    table_rows = 3 * combo_total
    dom_width = dom_sends.shape[1]
    sec_width = sector_sends.shape[1]
    flat_shapes = mode_shapes.reshape(modes_total, 3 * node_total)
    displaced = jnp.dot(
        amplitudes, flat_shapes, precision=lax.Precision.HIGHEST, preferred_element_type=jnp.float32
    ).reshape(table_rows, node_total)
    dom_ext = padded(take_slots(displaced, dom_sends), (("dom", 1),), dom_width, False)
    sec_ext = padded(take_slots(displaced, sector_sends), (("sector", 1),), sec_width, True)
    halo_moved = jnp.concatenate(
        [outer_ends(dom_ext, dom_width), outer_ends(sec_ext, sec_width)], axis=1
    )
    extended = jnp.concatenate([displaced, halo_moved], axis=1)
    ext_width = extended.shape[1]
    elem_total = connectivity.shape[1]
    block_size = math.gcd(elem_total, 256)
    turn_total = elem_total // block_size

    def one_block(turn_index, forces):
        first_col = turn_index * block_size
        connect_block = lax.dynamic_slice_in_dim(connectivity, first_col, block_size, 1)
        grads_block = lax.dynamic_slice_in_dim(shape_grads, first_col, block_size, 2)
        lame_block = lax.dynamic_slice_in_dim(lame_params, first_col, block_size, 1)
        return element_forces(forces, extended, connect_block, grads_block, lame_block)

    slot_forces = lax.fori_loop(
        0, turn_total, one_block, jnp.zeros((table_rows, ext_width), jnp.float32)
    )
    own_forces = slot_forces[:, :node_total]
    dom_back = slot_forces[:, node_total : node_total + 2 * dom_width]
    sec_back = slot_forces[:, node_total + 2 * dom_width :]
    dom_return = padded(dom_back, (("dom", 1),), dom_width, False)
    own_forces = add_slots(own_forces, dom_sends, outer_ends(dom_return, dom_width))
    sec_return = padded(sec_back, (("sector", 1),), sec_width, True)
    own_forces = add_slots(own_forces, sector_sends, outer_ends(sec_return, sec_width))
    partial_modal = lax.dot_general(
        own_forces.reshape(combo_total, 3 * node_total),
        flat_shapes,
        (((1,), (1,)), ((), ())),
        precision=lax.Precision.HIGHEST,
        preferred_element_type=jnp.float32,
    )
    modal_total = lax.psum(partial_modal, ("sector", "dom"))
    all_nodes = node_total * lax.axis_size("sector") * lax.axis_size("dom")
    return (
        own_forces.reshape(combo_total, 3, node_total),
        modal_total / math.sqrt(3.0 * all_nodes),
    )


def solution(mesh):
    placed = (
        P(),
        P(None, None, ("sector", "dom")),
        P(None, None, ("sector", "dom")),
        P(None, ("sector", "dom")),
        P(None, ("sector", "dom")),
        P(None, ("sector", "dom")),
        P(None, ("sector", "dom")),
    )
    return jax.shard_map(
        local,
        mesh=mesh,
        in_specs=placed,
        out_specs=(P(None, None, ("sector", "dom")), P()),
        check_vma=False,
    )
```

profile of v0, /device:TPU:1, one launch (start us, length us, event | category | flops | bytes accessed | tf_op | source)
XLA Modules:
  0.0 308.0 jit_solution(2652404135059010113)
XLA Ops:
  2.1 1.1 copy.105
  5.3 1.6 gather_fusion.1
  7.1 5.5 %collective-permute-start = (f32[192,256]{0,1:T(8,128)S(1)}, f32[192,256]{0,1:T(8,128)S(1)}, u32[]{:S(2)}, u32[]{:S(2)}) collective-permute-start(f32[192,256]{0,1:T(8,128)S(1)} %get-tuple-element.244), channel_id=1, source_target_pairs={{0,1},{1,2},{2,3},{3,4},{4,5},{5,6},{6,7},{7,8},{8,9},{9,10},{10,1... | collective-permute-start | bytes 589832 | tf_op jit(solution)/shard_map/ppermute | solution.py:16
  12.6 1.0 gather_fusion.2
  13.7 4.6 %collective-permute-start.3 = (f32[192,128]{0,1:T(8,128)S(1)}, f32[192,128]{0,1:T(8,128)S(1)}, u32[]{:S(2)}, u32[]{:S(2)}) collective-permute-start(f32[192,128]{0,1:T(8,128)S(1)} %get-tuple-element.245), channel_id=1, source_target_pairs={{32,0},{64,32},{96,64},{128,96},{160,128},{192,160},{224,192},{256... | collective-permute-start | bytes 294920 | tf_op jit(solution)/shard_map/ppermute | solution.py:18
  18.4 1.9 collective-permute-start.2
  20.3 1.5 collective-permute-start.1
  21.9 9.2 %collective-permute-done.1 = f32[192,256]{0,1:T(8,128)S(1)} collective-permute-done((f32[192,256]{0,1:T(8,128)S(1)}, f32[192,256]{0,1:T(8,128)S(1)}, u32[]{:S(2)}, u32[]{:S(2)}) %collective-permute-start.1) | collective-permute-done | bytes 196640 | tf_op jit(solution)/shard_map/ppermute | solution.py:18
  31.3 1.1 copy-done.1
  32.4 136.4 %while.15 = (s32[]{:T(128)}, f32[192,1792]{0,1:T(8,128)S(1)}, s32[8,1024]{1,0:T(8,128)S(1)}, f32[2,1024]{1,0:T(2,128)}, f32[192,1792]{0,1:T(8,128)}, /*index=5*/...) while((s32[]{:T(128)}, f32[192,1792]{0,1:T(8,128)S(1)}, ...), condition=%wide.region_12.13_spmd, body=%wide.region_0.12_spmd.sunk | while | flops 12415007 | bytes 49229240 | solution.py:95
  33.3 1.3 constant_dynamic-slice_fusion.11
  34.6 10.1 %gather_fusion = f32[2048,192]{1,0:T(8,128)} fusion(f32[192,1792]{0,1:T(8,128)} %get-tuple-element.414, s32[2048]{0:T(1024)S(1)} %broadcast_clamp_fusion.2), kind=kCustom, calls=%fused_computation.clone.1 | custom fusion | bytes 3153920 | tf_op jit(solution)/shard_map/while/body/eval_jaxpr/jit(_take)/gather | solution.py:42
  44.7 1.9 copy.147
  47.3 1.1 fusion.28
  50.4 0.9 copy.149
  51.9 1.8 copy.151
  53.8 12.6 %scatter_fusion = f32[192,1792]{0,1:T(8,128)S(1)} fusion(f32[192,1792]{0,1:T(8,128)S(1)} %get-tuple-element.394, s32[2048]{0:T(1024)S(1)} %bitcast.158, f32[2048,192]{1,0:T(8,128)} %copy.151), kind=kCustom, calls=%fused_computation.3.clone.1 | custom fusion | flops 393216 | bytes 4726784 | tf_op jit(solution)/shard_map/while/body/eval_jaxpr/scatter-add | solution.py:58
  67.4 1.4 constant_dynamic-slice_fusion.11
  68.8 10.1 %gather_fusion = f32[2048,192]{1,0:T(8,128)} fusion(f32[192,1792]{0,1:T(8,128)} %get-tuple-element.414, s32[2048]{0:T(1024)S(1)} %broadcast_clamp_fusion.2), kind=kCustom, calls=%fused_computation.clone.1 | custom fusion | bytes 3153920 | tf_op jit(solution)/shard_map/while/body/eval_jaxpr/jit(_take)/gather | solution.py:42
  78.8 1.9 copy.147
  81.4 1.1 fusion.28
  84.5 0.9 copy.149
  86.0 1.8 copy.151
  87.9 12.6 %scatter_fusion = f32[192,1792]{0,1:T(8,128)S(1)} fusion(f32[192,1792]{0,1:T(8,128)S(1)} %get-tuple-element.394, s32[2048]{0:T(1024)S(1)} %bitcast.158, f32[2048,192]{1,0:T(8,128)} %copy.151), kind=kCustom, calls=%fused_computation.3.clone.1 | custom fusion | flops 393216 | bytes 4726784 | tf_op jit(solution)/shard_map/while/body/eval_jaxpr/scatter-add | solution.py:58
  101.5 1.3 constant_dynamic-slice_fusion.11
  102.8 10.1 %gather_fusion = f32[2048,192]{1,0:T(8,128)} fusion(f32[192,1792]{0,1:T(8,128)} %get-tuple-element.414, s32[2048]{0:T(1024)S(1)} %broadcast_clamp_fusion.2), kind=kCustom, calls=%fused_computation.clone.1 | custom fusion | bytes 3153920 | tf_op jit(solution)/shard_map/while/body/eval_jaxpr/jit(_take)/gather | solution.py:42
  112.9 1.9 copy.147
  115.5 1.1 fusion.28
  118.6 0.9 copy.149
  120.1 1.8 copy.151
  122.0 12.6 %scatter_fusion = f32[192,1792]{0,1:T(8,128)S(1)} fusion(f32[192,1792]{0,1:T(8,128)S(1)} %get-tuple-element.394, s32[2048]{0:T(1024)S(1)} %bitcast.158, f32[2048,192]{1,0:T(8,128)} %copy.151), kind=kCustom, calls=%fused_computation.3.clone.1 | custom fusion | flops 393216 | bytes 4726784 | tf_op jit(solution)/shard_map/while/body/eval_jaxpr/scatter-add | solution.py:58
  135.6 1.4 constant_dynamic-slice_fusion.11
  137.0 10.1 %gather_fusion = f32[2048,192]{1,0:T(8,128)} fusion(f32[192,1792]{0,1:T(8,128)} %get-tuple-element.414, s32[2048]{0:T(1024)S(1)} %broadcast_clamp_fusion.2), kind=kCustom, calls=%fused_computation.clone.1 | custom fusion | bytes 3153920 | tf_op jit(solution)/shard_map/while/body/eval_jaxpr/jit(_take)/gather | solution.py:42
  147.0 1.9 copy.147
  149.6 1.1 fusion.28
  152.7 0.9 copy.149
  154.2 1.8 copy.151
  156.1 12.6 %scatter_fusion = f32[192,1792]{0,1:T(8,128)S(1)} fusion(f32[192,1792]{0,1:T(8,128)S(1)} %get-tuple-element.394, s32[2048]{0:T(1024)S(1)} %bitcast.158, f32[2048,192]{1,0:T(8,128)} %copy.151), kind=kCustom, calls=%fused_computation.3.clone.1 | custom fusion | flops 393216 | bytes 4726784 | tf_op jit(solution)/shard_map/while/body/eval_jaxpr/scatter-add | solution.py:58
  168.8 2.8 collective-permute-start.4
  171.6 1.3 collective-permute-start.5
  173.6 4.8 %collective-permute-start.6 = (f32[192,128]{0,1:T(8,128)}, f32[192,128]{0,1:T(8,128)}, u32[]{:S(2)}, u32[]{:S(2)}) collective-permute-start(f32[192,128]{0,1:T(8,128)} %get-tuple-element.239), channel_id=1, source_target_pairs={{0,32},{32,64},{64,96},{96,128},{128,160},{160,192},{192,224},{224... | collective-permute-start | bytes 294920 | tf_op jit(solution)/shard_map/ppermute | solution.py:16
  178.4 2.2 collective-permute-start.7
  180.7 3.8 %scatter_custom_fusion.1 = f32[192,1024]{0,1:T(8,128)S(1)} fusion(f32[192,1024]{0,1:T(8,128)S(1)} %slice.257, s32[512]{0:T(512)S(1)} %bitcast.167, f32[192,256]{0,1:T(8,128)S(1)} %collective-permute-done.5, f32[]{:T(128)} %constant.154, f32[192,256]{0,1:T(8,128)S(1)} %collective-permute-done.4), kind=kCustom, calls=%fused_computation.67 | custom fusion | flops 196608 | bytes 1310724 | tf_op jit(solution)/shard_map/scatter-add | solution.py:34
  184.5 0.9 collective-permute-done.6
  185.4 4.3 %collective-permute-done.7 = f32[192,128]{0,1:T(8,128)} collective-permute-done((f32[192,128]{0,1:T(8,128)}, f32[192,128]{0,1:T(8,128)}, u32[]{:S(2)}, u32[]{:S(2)}) %collective-permute-start.7) | collective-permute-done | bytes 98336 | tf_op jit(solution)/shard_map/ppermute | solution.py:18
  189.6 3.0 scatter_custom_fusion.2
  194.8 111.2 %psum.7 = f32[64,48]{0,1:T(8,128)S(1)} all-reduce(f32[64,48]{0,1:T(8,128)S(1)} %fusion.18), channel_id=1, replica_groups=mesh['sector'=16,'dom'=32] {'sector','dom'}, use_global_device_ids=true, to_apply=%region_15.16 | all-reduce | flops 3072 | bytes 24576 | tf_op jit(solution)/shard_map/psum | solution.py:112
  306.6 1.3 copy.92
  (178 shorter events, 24.1 us)
Async XLA Ops:
  0.6 3.4 %copy-start = (f32[64,48]{0,1:T(8,128)S(1)}, f32[64,48]{0,1:T(8,128)}, u32[]{:S(2)}) copy-start(f32[64,48]{0,1:T(8,128)} %param.9) | copy-start | bytes 36868
  3.2 0.8 copy-start.2
  6.9 5.7 %copy-start.5 = (s32[2,128]{1,0:T(2,128)S(1)}, s32[2,128]{1,0:T(2,128)}, u32[]{:S(2)}) copy-start(s32[2,128]{1,0:T(2,128)} %param.15) | copy-start | bytes 3076
  7.1 14.8 %collective-permute-start = (f32[192,256]{0,1:T(8,128)S(1)}, f32[192,256]{0,1:T(8,128)S(1)}, u32[]{:S(2)}, u32[]{:S(2)}) collective-permute-start(f32[192,256]{0,1:T(8,128)S(1)} %get-tuple-element.244), channel_id=1, source_target_pairs={{0,1},{1,2},{2,3},{3,4},{4,5},{5,6},{6,7},{7,8},{8,9},{9,10},{10,1... | collective-permute-start | bytes 589832 | tf_op jit(solution)/shard_map/ppermute | solution.py:16
  13.7 17.4 %collective-permute-start.3 = (f32[192,128]{0,1:T(8,128)S(1)}, f32[192,128]{0,1:T(8,128)S(1)}, u32[]{:S(2)}, u32[]{:S(2)}) collective-permute-start(f32[192,128]{0,1:T(8,128)S(1)} %get-tuple-element.245), channel_id=1, source_target_pairs={{32,0},{64,32},{96,64},{128,96},{160,128},{192,160},{224,192},{256... | collective-permute-start | bytes 294920 | tf_op jit(solution)/shard_map/ppermute | solution.py:18
  18.4 12.7 %collective-permute-start.2 = (f32[192,128]{0,1:T(8,128)S(1)}, f32[192,128]{0,1:T(8,128)S(1)}, u32[]{:S(2)}, u32[]{:S(2)}) collective-permute-start(f32[192,128]{0,1:T(8,128)S(1)} %get-tuple-element.246), channel_id=1, source_target_pairs={{0,32},{32,64},{64,96},{96,128},{128,160},{160,192},{192,224},{224... | collective-permute-start | bytes 294920 | tf_op jit(solution)/shard_map/ppermute | solution.py:16
  20.3 10.8 %collective-permute-start.1 = (f32[192,256]{0,1:T(8,128)S(1)}, f32[192,256]{0,1:T(8,128)S(1)}, u32[]{:S(2)}, u32[]{:S(2)}) collective-permute-start(f32[192,256]{0,1:T(8,128)S(1)} %get-tuple-element.243), channel_id=1, source_target_pairs={{1,0},{2,1},{3,2},{4,3},{5,4},{6,5},{7,6},{8,7},{9,8},{10,9},{11,1... | collective-permute-start | bytes 589832 | tf_op jit(solution)/shard_map/ppermute | solution.py:18
  21.9 10.5 %copy-start.4 = (s32[8,1024]{1,0:T(8,128)S(1)}, s32[8,1024]{1,0:T(8,128)}, u32[]{:S(2)}) copy-start(s32[8,1024]{1,0:T(8,128)} %param.13) | copy-start | bytes 98308
  31.1 1.2 copy-start.1
  168.8 11.9 %collective-permute-start.4 = (f32[192,256]{0,1:T(8,128)S(1)}, f32[192,256]{0,1:T(8,128)S(1)}, u32[]{:S(2)}, u32[]{:S(2)}) collective-permute-start(f32[192,256]{0,1:T(8,128)S(1)} %get-tuple-element.241), channel_id=1, source_target_pairs={{0,1},{1,2},{2,3},{3,4},{4,5},{5,6},{6,7},{7,8},{8,9},{9,10},{10,1... | collective-permute-start | bytes 589832 | tf_op jit(solution)/shard_map/ppermute | solution.py:16
  171.6 9.1 %collective-permute-start.5 = (f32[192,256]{0,1:T(8,128)S(1)}, f32[192,256]{0,1:T(8,128)S(1)}, u32[]{:S(2)}, u32[]{:S(2)}) collective-permute-start(f32[192,256]{0,1:T(8,128)S(1)} %get-tuple-element.242), channel_id=1, source_target_pairs={{1,0},{2,1},{3,2},{4,3},{5,4},{6,5},{7,6},{8,7},{9,8},{10,9},{11,1... | collective-permute-start | bytes 589832 | tf_op jit(solution)/shard_map/ppermute | solution.py:18
  173.6 11.8 %collective-permute-start.6 = (f32[192,128]{0,1:T(8,128)}, f32[192,128]{0,1:T(8,128)}, u32[]{:S(2)}, u32[]{:S(2)}) collective-permute-start(f32[192,128]{0,1:T(8,128)} %get-tuple-element.239), channel_id=1, source_target_pairs={{0,32},{32,64},{64,96},{96,128},{128,160},{160,192},{192,224},{224... | collective-permute-start | bytes 294920 | tf_op jit(solution)/shard_map/ppermute | solution.py:16
  178.4 11.3 %collective-permute-start.7 = (f32[192,128]{0,1:T(8,128)}, f32[192,128]{0,1:T(8,128)}, u32[]{:S(2)}, u32[]{:S(2)}) collective-permute-start(f32[192,128]{0,1:T(8,128)} %get-tuple-element.240), channel_id=1, source_target_pairs={{32,0},{64,32},{96,64},{128,96},{160,128},{192,160},{224,192},{256... | collective-permute-start | bytes 294920 | tf_op jit(solution)/shard_map/ppermute | solution.py:18
  193.0 1.1 copy-start.3
where the time goes:
time: 309 us; the launch traced here: 308 us
  blocking collectives  111 us (36%)
  local copies, waits for them, and re-layouts  87.5 us (28%)
  other arithmetic  66.7 us (22%)
  starting transfers between devices  24.6 us (8%)
  waiting for transfers between devices  14.3 us (5%)
    psum x1, blocking collectives, local(): modal_total = lax.psum(partial_modal, ('sector', 'dom'))  111 us
    scatter-add x4, other arithmetic, element_forces(): accum.at[:, slot_index]  50.6 us
    gather x8, local copies, waits for them, and re-layouts, element_forces(): jnp.take(extended, slot_index, axis=1, mode='fill', fill_value=0.0)  47.8 us
    ppermute x4, starting transfers between devices, padded(): lax.ppermute(tail, axis, [(i, (i + 1) % count) for i in range(ends)])  15 us
    ppermute x4, waiting for transfers between devices, padded(): lax.ppermute(head, axis, [((i + 1) % count, i) for i in range(ends)])  13.4 us
    ppermute x4, starting transfers between devices, padded(): lax.ppermute(head, axis, [((i + 1) % count, i) for i in range(ends)])  9.62 us
    reshape x4, local copies, waits for them, and re-layouts, element_forces(): corner_forces.reshape(3 * combo_total, 8 * elem_total)  7.39 us
    scatter-add x2, other arithmetic, add_slots(): return node_table.at[:, slot_index].add(add_values, mode='drop')  6.78 us
  transfers between devices with their start and end apart: 8, of which 3 were waited for; matrix products, arithmetic and copies ran while one was open for 2% of the time, Pallas kernels for 0%

commit v1 on v0

--- a/solution.py
+++ b/solution.py
@@ -109,7 +109,9 @@
         precision=lax.Precision.HIGHEST,
         preferred_element_type=jnp.float32,
     )
-    modal_total = lax.psum(partial_modal, ("sector", "dom"))
+    modal_total = partial_modal
+    for over in ("sector", "dom"):
+        modal_total = lax.psum(modal_total, over)
     all_nodes = node_total * lax.axis_size("sector") * lax.axis_size("dom")
     return (
         own_forces.reshape(combo_total, 3, node_total),

time: 309 us -> 403 us (1.30)
  the two profiles are of different devices: /device:TPU:1 before, /device:TPU:32 now
where the time goes in v1:
time: 403 us; the launch traced here: 401 us
  blocking collectives  204 us (51%)
  local copies, waits for them, and re-layouts  87.5 us (22%)
  other arithmetic  66.7 us (17%)
  starting transfers between devices  31.9 us (8%)
  waiting for transfers between devices  7.5 us (2%)
    psum x2, blocking collectives, local(): modal_total = lax.psum(modal_total, over)  204 us
    scatter-add x4, other arithmetic, element_forces(): accum.at[:, slot_index]  50.6 us
    gather x8, local copies, waits for them, and re-layouts, element_forces(): jnp.take(extended, slot_index, axis=1, mode='fill', fill_value=0.0)  47.8 us
    ppermute x4, starting transfers between devices, padded(): lax.ppermute(head, axis, [((i + 1) % count, i) for i in range(ends)])  17.9 us
    ppermute x4, starting transfers between devices, padded(): lax.ppermute(tail, axis, [(i, (i + 1) % count) for i in range(ends)])  13.9 us
  transfers between devices with their start and end apart: 8, of which 3 were waited for; matrix products, arithmetic and copies ran while one was open for 1% of the time, Pallas kernels for 0%

profile of v1, /device:TPU:32, one launch (start us, length us, event | category | flops | bytes accessed | tf_op | source)
XLA Modules:
  0.0 401.2 jit_solution(17959535056522913990)
XLA Ops:
  2.1 1.1 copy.105
  5.3 1.6 gather_fusion.1
  7.1 4.9 %collective-permute-start = (f32[192,256]{0,1:T(8,128)S(1)}, f32[192,256]{0,1:T(8,128)S(1)}, u32[]{:S(2)}, u32[]{:S(2)}) collective-permute-start(f32[192,256]{0,1:T(8,128)S(1)} %get-tuple-element.244), channel_id=1, source_target_pairs={{0,1},{1,2},{2,3},{3,4},{4,5},{5,6},{6,7},{7,8},{8,9},{9,10},{10,1... | collective-permute-start | bytes 589832 | tf_op jit(solution)/shard_map/ppermute | solution.py:16
  12.1 1.0 gather_fusion.2
  13.2 4.1 %collective-permute-start.3 = (f32[192,128]{0,1:T(8,128)S(1)}, f32[192,128]{0,1:T(8,128)S(1)}, u32[]{:S(2)}, u32[]{:S(2)}) collective-permute-start(f32[192,128]{0,1:T(8,128)S(1)} %get-tuple-element.245), channel_id=1, source_target_pairs={{32,0},{64,32},{96,64},{128,96},{160,128},{192,160},{224,192},{256... | collective-permute-start | bytes 294920 | tf_op jit(solution)/shard_map/ppermute | solution.py:18
  17.3 1.9 collective-permute-start.2
  19.2 5.0 %collective-permute-start.1 = (f32[192,256]{0,1:T(8,128)S(1)}, f32[192,256]{0,1:T(8,128)S(1)}, u32[]{:S(2)}, u32[]{:S(2)}) collective-permute-start(f32[192,256]{0,1:T(8,128)S(1)} %get-tuple-element.243), channel_id=1, source_target_pairs={{1,0},{2,1},{3,2},{4,3},{5,4},{6,5},{7,6},{8,7},{9,8},{10,9},{11,1... | collective-permute-start | bytes 589832 | tf_op jit(solution)/shard_map/ppermute | solution.py:18
  24.4 6.0 %collective-permute-done.1 = f32[192,256]{0,1:T(8,128)S(1)} collective-permute-done((f32[192,256]{0,1:T(8,128)S(1)}, f32[192,256]{0,1:T(8,128)S(1)}, u32[]{:S(2)}, u32[]{:S(2)}) %collective-permute-start.1) | collective-permute-done | bytes 196640 | tf_op jit(solution)/shard_map/ppermute | solution.py:18
  30.6 1.1 copy-done.1
  31.7 136.4 %while.15 = (s32[]{:T(128)}, f32[192,1792]{0,1:T(8,128)S(1)}, s32[8,1024]{1,0:T(8,128)S(1)}, f32[2,1024]{1,0:T(2,128)}, f32[192,1792]{0,1:T(8,128)}, /*index=5*/...) while((s32[]{:T(128)}, f32[192,1792]{0,1:T(8,128)S(1)}, ...), condition=%wide.region_12.13_spmd, body=%wide.region_0.12_spmd.sunk | while | flops 12415007 | bytes 49229240 | solution.py:95
  32.6 1.3 constant_dynamic-slice_fusion.11
  33.9 10.1 %gather_fusion = f32[2048,192]{1,0:T(8,128)} fusion(f32[192,1792]{0,1:T(8,128)} %get-tuple-element.414, s32[2048]{0:T(1024)S(1)} %broadcast_clamp_fusion.2), kind=kCustom, calls=%fused_computation.clone.1 | custom fusion | bytes 3153920 | tf_op jit(solution)/shard_map/while/body/eval_jaxpr/jit(_take)/gather | solution.py:42
  44.0 1.9 copy.147
  46.6 1.1 fusion.28
  49.7 0.9 copy.149
  51.2 1.8 copy.151
  53.1 12.6 %scatter_fusion = f32[192,1792]{0,1:T(8,128)S(1)} fusion(f32[192,1792]{0,1:T(8,128)S(1)} %get-tuple-element.394, s32[2048]{0:T(1024)S(1)} %bitcast.158, f32[2048,192]{1,0:T(8,128)} %copy.151), kind=kCustom, calls=%fused_computation.3.clone.1 | custom fusion | flops 393216 | bytes 4726784 | tf_op jit(solution)/shard_map/while/body/eval_jaxpr/scatter-add | solution.py:58
  66.7 1.4 constant_dynamic-slice_fusion.11
  68.1 10.1 %gather_fusion = f32[2048,192]{1,0:T(8,128)} fusion(f32[192,1792]{0,1:T(8,128)} %get-tuple-element.414, s32[2048]{0:T(1024)S(1)} %broadcast_clamp_fusion.2), kind=kCustom, calls=%fused_computation.clone.1 | custom fusion | bytes 3153920 | tf_op jit(solution)/shard_map/while/body/eval_jaxpr/jit(_take)/gather | solution.py:42
  78.1 1.9 copy.147
  80.7 1.1 fusion.28
  83.8 0.9 copy.149
  85.3 1.8 copy.151
  87.2 12.6 %scatter_fusion = f32[192,1792]{0,1:T(8,128)S(1)} fusion(f32[192,1792]{0,1:T(8,128)S(1)} %get-tuple-element.394, s32[2048]{0:T(1024)S(1)} %bitcast.158, f32[2048,192]{1,0:T(8,128)} %copy.151), kind=kCustom, calls=%fused_computation.3.clone.1 | custom fusion | flops 393216 | bytes 4726784 | tf_op jit(solution)/shard_map/while/body/eval_jaxpr/scatter-add | solution.py:58
  100.8 1.3 constant_dynamic-slice_fusion.11
  102.1 10.1 %gather_fusion = f32[2048,192]{1,0:T(8,128)} fusion(f32[192,1792]{0,1:T(8,128)} %get-tuple-element.414, s32[2048]{0:T(1024)S(1)} %broadcast_clamp_fusion.2), kind=kCustom, calls=%fused_computation.clone.1 | custom fusion | bytes 3153920 | tf_op jit(solution)/shard_map/while/body/eval_jaxpr/jit(_take)/gather | solution.py:42
  112.2 1.9 copy.147
  114.8 1.1 fusion.28
  117.9 0.9 copy.149
  119.4 1.8 copy.151
  121.3 12.6 %scatter_fusion = f32[192,1792]{0,1:T(8,128)S(1)} fusion(f32[192,1792]{0,1:T(8,128)S(1)} %get-tuple-element.394, s32[2048]{0:T(1024)S(1)} %bitcast.158, f32[2048,192]{1,0:T(8,128)} %copy.151), kind=kCustom, calls=%fused_computation.3.clone.1 | custom fusion | flops 393216 | bytes 4726784 | tf_op jit(solution)/shard_map/while/body/eval_jaxpr/scatter-add | solution.py:58
  134.9 1.4 constant_dynamic-slice_fusion.11
  136.3 10.1 %gather_fusion = f32[2048,192]{1,0:T(8,128)} fusion(f32[192,1792]{0,1:T(8,128)} %get-tuple-element.414, s32[2048]{0:T(1024)S(1)} %broadcast_clamp_fusion.2), kind=kCustom, calls=%fused_computation.clone.1 | custom fusion | bytes 3153920 | tf_op jit(solution)/shard_map/while/body/eval_jaxpr/jit(_take)/gather | solution.py:42
  146.3 1.9 copy.147
  148.9 1.1 fusion.28
  152.0 0.9 copy.149
  153.5 1.8 copy.151
  155.4 12.6 %scatter_fusion = f32[192,1792]{0,1:T(8,128)S(1)} fusion(f32[192,1792]{0,1:T(8,128)S(1)} %get-tuple-element.394, s32[2048]{0:T(1024)S(1)} %bitcast.158, f32[2048,192]{1,0:T(8,128)} %copy.151), kind=kCustom, calls=%fused_computation.3.clone.1 | custom fusion | flops 393216 | bytes 4726784 | tf_op jit(solution)/shard_map/while/body/eval_jaxpr/scatter-add | solution.py:58
  168.1 5.2 %collective-permute-start.4 = (f32[192,256]{0,1:T(8,128)S(1)}, f32[192,256]{0,1:T(8,128)S(1)}, u32[]{:S(2)}, u32[]{:S(2)}) collective-permute-start(f32[192,256]{0,1:T(8,128)S(1)} %get-tuple-element.241), channel_id=1, source_target_pairs={{0,1},{1,2},{2,3},{3,4},{4,5},{5,6},{6,7},{7,8},{8,9},{9,10},{10,1... | collective-permute-start | bytes 589832 | tf_op jit(solution)/shard_map/ppermute | solution.py:16
  173.3 3.1 collective-permute-start.5
  177.1 1.9 collective-permute-start.6
  179.0 5.8 %collective-permute-start.7 = (f32[192,128]{0,1:T(8,128)}, f32[192,128]{0,1:T(8,128)}, u32[]{:S(2)}, u32[]{:S(2)}) collective-permute-start(f32[192,128]{0,1:T(8,128)} %get-tuple-element.240), channel_id=1, source_target_pairs={{32,0},{64,32},{96,64},{128,96},{160,128},{192,160},{224,192},{256... | collective-permute-start | bytes 294920 | tf_op jit(solution)/shard_map/ppermute | solution.py:18
  184.8 1.1 collective-permute-done.5
  185.9 3.7 scatter_custom_fusion.1
  190.1 3.0 scatter_custom_fusion.2
  195.3 55.9 %psum.14 = f32[64,48]{0,1:T(8,128)S(1)} all-reduce(f32[64,48]{0,1:T(8,128)S(1)} %fusion.18), channel_id=1, replica_groups=mesh['sector'=16,'dom'=32] {'sector'}, use_global_device_ids=true, to_apply=%region_15.16 | all-reduce | flops 3072 | bytes 24576 | tf_op jit(solution)/shard_map/psum | solution.py:114
  251.1 148.1 %psum.15 = f32[64,48]{0,1:T(8,128)S(1)} all-reduce(f32[64,48]{0,1:T(8,128)S(1)} %psum.14), channel_id=1, replica_groups=mesh['sector'=16,'dom'=32] {'dom'}, use_global_device_ids=true, to_apply=%region_16.17 | all-reduce | flops 3072 | bytes 24576 | tf_op jit(solution)/shard_map/psum | solution.py:114
  399.8 1.3 copy.92
  (179 shorter events, 24.5 us)
Async XLA Ops:
  0.6 3.4 copy-start
  3.2 0.8 copy-start.2
  6.9 5.2 %copy-start.5 = (s32[2,128]{1,0:T(2,128)S(1)}, s32[2,128]{1,0:T(2,128)}, u32[]{:S(2)}) copy-start(s32[2,128]{1,0:T(2,128)} %param.15) | copy-start | bytes 3076
  7.1 17.2 %collective-permute-start = (f32[192,256]{0,1:T(8,128)S(1)}, f32[192,256]{0,1:T(8,128)S(1)}, u32[]{:S(2)}, u32[]{:S(2)}) collective-permute-start(f32[192,256]{0,1:T(8,128)S(1)} %get-tuple-element.244), channel_id=1, source_target_pairs={{0,1},{1,2},{2,3},{3,4},{4,5},{5,6},{6,7},{7,8},{8,9},{9,10},{10,1... | collective-permute-start | bytes 589832 | tf_op jit(solution)/shard_map/ppermute | solution.py:16
  13.2 17.2 %collective-permute-start.3 = (f32[192,128]{0,1:T(8,128)S(1)}, f32[192,128]{0,1:T(8,128)S(1)}, u32[]{:S(2)}, u32[]{:S(2)}) collective-permute-start(f32[192,128]{0,1:T(8,128)S(1)} %get-tuple-element.245), channel_id=1, source_target_pairs={{32,0},{64,32},{96,64},{128,96},{160,128},{192,160},{224,192},{256... | collective-permute-start | bytes 294920 | tf_op jit(solution)/shard_map/ppermute | solution.py:18
  17.3 13.1 %collective-permute-start.2 = (f32[192,128]{0,1:T(8,128)S(1)}, f32[192,128]{0,1:T(8,128)S(1)}, u32[]{:S(2)}, u32[]{:S(2)}) collective-permute-start(f32[192,128]{0,1:T(8,128)S(1)} %get-tuple-element.246), channel_id=1, source_target_pairs={{0,32},{32,64},{64,96},{96,128},{128,160},{160,192},{192,224},{224... | collective-permute-start | bytes 294920 | tf_op jit(solution)/shard_map/ppermute | solution.py:16
  19.2 11.1 %collective-permute-start.1 = (f32[192,256]{0,1:T(8,128)S(1)}, f32[192,256]{0,1:T(8,128)S(1)}, u32[]{:S(2)}, u32[]{:S(2)}) collective-permute-start(f32[192,256]{0,1:T(8,128)S(1)} %get-tuple-element.243), channel_id=1, source_target_pairs={{1,0},{2,1},{3,2},{4,3},{5,4},{6,5},{7,6},{8,7},{9,8},{10,9},{11,1... | collective-permute-start | bytes 589832 | tf_op jit(solution)/shard_map/ppermute | solution.py:18
  24.3 7.4 %copy-start.4 = (s32[8,1024]{1,0:T(8,128)S(1)}, s32[8,1024]{1,0:T(8,128)}, u32[]{:S(2)}) copy-start(s32[8,1024]{1,0:T(8,128)} %param.13) | copy-start | bytes 98308
  30.4 1.2 copy-start.1
  168.1 16.7 %collective-permute-start.4 = (f32[192,256]{0,1:T(8,128)S(1)}, f32[192,256]{0,1:T(8,128)S(1)}, u32[]{:S(2)}, u32[]{:S(2)}) collective-permute-start(f32[192,256]{0,1:T(8,128)S(1)} %get-tuple-element.241), channel_id=1, source_target_pairs={{0,1},{1,2},{2,3},{3,4},{4,5},{5,6},{6,7},{7,8},{8,9},{9,10},{10,1... | collective-permute-start | bytes 589832 | tf_op jit(solution)/shard_map/ppermute | solution.py:16
  173.3 12.6 %collective-permute-start.5 = (f32[192,256]{0,1:T(8,128)S(1)}, f32[192,256]{0,1:T(8,128)S(1)}, u32[]{:S(2)}, u32[]{:S(2)}) collective-permute-start(f32[192,256]{0,1:T(8,128)S(1)} %get-tuple-element.242), channel_id=1, source_target_pairs={{1,0},{2,1},{3,2},{4,3},{5,4},{6,5},{7,6},{8,7},{9,8},{10,9},{11,1... | collective-permute-start | bytes 589832 | tf_op jit(solution)/shard_map/ppermute | solution.py:18
  177.1 13.0 %collective-permute-start.6 = (f32[192,128]{0,1:T(8,128)}, f32[192,128]{0,1:T(8,128)}, u32[]{:S(2)}, u32[]{:S(2)}) collective-permute-start(f32[192,128]{0,1:T(8,128)} %get-tuple-element.239), channel_id=1, source_target_pairs={{0,32},{32,64},{64,96},{96,128},{128,160},{160,192},{192,224},{224... | collective-permute-start | bytes 294920 | tf_op jit(solution)/shard_map/ppermute | solution.py:16
  179.0 11.1 %collective-permute-start.7 = (f32[192,128]{0,1:T(8,128)}, f32[192,128]{0,1:T(8,128)}, u32[]{:S(2)}, u32[]{:S(2)}) collective-permute-start(f32[192,128]{0,1:T(8,128)} %get-tuple-element.240), channel_id=1, source_target_pairs={{32,0},{64,32},{96,64},{128,96},{160,128},{192,160},{224,192},{256... | collective-permute-start | bytes 294920 | tf_op jit(solution)/shard_map/ppermute | solution.py:18
  193.4 1.1 copy-start.3
